TPU v7x, 32 devices: a whole 2x2x4 slice. The times are simulated.
32 devices in a mesh: seq: 8 (over y, x, core), fsdp: 4 (over z).
Axes of the slice: x: 2, y: 2, z: 4, core: 2. Of those that a mesh axis runs over, the one named last changes fastest.
Arguments:
- tokens: bfloat16 [4, 2048, 1536], P('fsdp', 'seq'), may hold values from -6 to 6
- segment_ids: int32 [4, 2048], P('fsdp'), may hold values from 0 to 7, never falling along the last dimension, each value on 1 to 512 neighbouring positions
- cotangent: bfloat16 [4, 2048, 1536], P('fsdp', 'seq'), may hold values from -6 to 6
- w_in: bfloat16 [1536, 6448], P('fsdp'), may hold values from -0.15625 to 0.15625
- w_out: bfloat16 [3072, 1536], P('fsdp'), may hold values from -0.109375 to 0.109375
- conv_w: bfloat16 [4, 3328], P(None, 'fsdp'), may hold values from -3 to 3
- conv_b: bfloat16 [3328], P('fsdp'), may hold values from -1.5 to 1.5
- a_log: bfloat16 [48], P('fsdp'), may hold values from -3 to 1.5
- dt_bias: bfloat16 [48], P('fsdp'), may hold values from -5.5 to -3
- d_skip: bfloat16 [48], P('fsdp'), may hold values from 0.5 to 1.5
- norm_w: bfloat16 [1536], P('fsdp'), may hold values from 0.5 to 1.5
- gate_w: bfloat16 [3072], P('fsdp'), may hold values from 0.5 to 1.5
Outputs:
- layer_out: bfloat16 [4, 2048, 1536], P('fsdp', 'seq')
- token_grad: float32 [4, 2048, 1536], P('fsdp', 'seq')
- w_in_grad: float32 [1536, 6448], P('fsdp')
- w_out_grad: float32 [3072, 1536], P('fsdp')
- conv_w_grad: float32 [4, 3328], P(None, 'fsdp')
- conv_b_grad: float32 [3328], P('fsdp')
- a_log_grad: float32 [48], P('fsdp')
- dt_bias_grad: float32 [48], P('fsdp')
- d_skip_grad: float32 [48], P('fsdp')
- norm_w_grad: float32 [1536], P('fsdp')
- gate_w_grad: float32 [3072], P('fsdp')
Inputs may be any that keep to these rules, and one draw needn't show every extreme that they name: `segment_ids`: in each sequence the ids never fall from one token to the next, start at 0 and take every value; each document has 1 to 512 tokens and one has exactly 512.
All inputs are finite; a program needn't handle non-finite values.
Results may differ from a plain program's by a relative error of at most 0.011.
Values may be sent and summed in bfloat16 or wider, within the bound.
A program may use at most 320 MiB of HBM per device.

v0:
```python
import jax
import jax.numpy as jnp
from jax import lax
from jax.sharding import PartitionSpec as P

DI = 3072
HEADDIM = 64
STATE = 128
CONV = 4
SPAN = 256
HEADS = 48
CHAN = 3328
EPSILON = 1e-05
HIGHEST = lax.Precision.HIGHEST


def passed_along(value, axis, steps):
    count = lax.axis_size(axis)
    first, last = (max(0, -steps), min(count, count - steps))
    return lax.ppermute(value, axis, [(source, source + steps) for source in range(first, last)])


def shortened(array):

    def short(part):
        return part.astype(jnp.bfloat16) if part.dtype == jnp.float32 else part

    return jax.tree.map(short, array)


def block_masks(ids_blocks, before_ids):
    block_len = ids_blocks.shape[1]
    places = jnp.arange(block_len)
    causal_mask = (places[:, None] >= places[None, :])[None] & (
        ids_blocks[:, :, None] == ids_blocks[:, None, :]
    )
    keep_flag = (ids_blocks == before_ids[:, None]).astype(jnp.float32)
    same_last = (ids_blocks == ids_blocks[:, -1:]).astype(jnp.float32)
    return (causal_mask, keep_flag, same_last)


def local_states(x_heads, b_rows, step_size, log_decay, same_last, keep_flag):
    cum_decay = jnp.cumsum(log_decay, axis=1)
    last_cum = cum_decay[:, -1]
    weights = jnp.exp(last_cum[:, None, :] - cum_decay) * step_size * same_last[:, :, None]
    fresh_state = jnp.einsum("csh,cshp,csn->chpn", weights, x_heads, b_rows, precision=HIGHEST)
    passing = keep_flag[:, -1:] * jnp.exp(last_cum)
    total_state = jnp.zeros_like(fresh_state[0])
    total_decay = jnp.ones_like(passing[0])
    total_state = fresh_state[0] + passing[0][:, None, None] * total_state
    total_decay = total_decay * passing[0]
    return (fresh_state, passing, total_state, total_decay)


def local_output(x_heads, b_rows, c_rows, step_size, log_decay, incoming, causal_mask, keep_flag):
    cum_decay = jnp.cumsum(log_decay, axis=1)
    cum_heads = jnp.swapaxes(cum_decay, 1, 2)
    gap_decay = cum_heads[:, :, :, None] - cum_heads[:, :, None, :]
    head_mask = causal_mask[:, None]
    decay_map = jnp.exp(jnp.where(head_mask, gap_decay, 0.0)) * head_mask.astype(jnp.float32)
    scores = jnp.einsum("ctn,csn->cts", c_rows, b_rows, precision=HIGHEST)
    mixing = scores[:, None] * decay_map * jnp.swapaxes(step_size, 1, 2)[:, :, None, :]
    inner_out = jnp.einsum("chts,cshp->cthp", mixing, x_heads, precision=HIGHEST)
    starts = [incoming]
    start_states = jnp.stack(starts)
    carried = jnp.einsum("ctn,chpn->cthp", c_rows, start_states, precision=HIGHEST)
    carried = carried * (keep_flag[:, :, None] * jnp.exp(cum_decay))[..., None]
    return inner_out + carried


def on_device(
    tokens,
    segment_ids,
    cotangent,
    w_in,
    w_out,
    conv_w,
    conv_b,
    a_log,
    dt_bias,
    d_skip,
    norm_w,
    gate_w,
):
    gathered = (
        lax.all_gather(w_in, "fsdp", axis=0, tiled=True),
        lax.all_gather(w_out, "fsdp", axis=0, tiled=True),
        lax.all_gather(conv_w, "fsdp", axis=1, tiled=True),
        lax.all_gather(conv_b, "fsdp", axis=0, tiled=True),
        lax.all_gather(a_log, "fsdp", axis=0, tiled=True),
        lax.all_gather(dt_bias, "fsdp", axis=0, tiled=True),
        lax.all_gather(d_skip, "fsdp", axis=0, tiled=True),
        lax.all_gather(norm_w, "fsdp", axis=0, tiled=True),
        lax.all_gather(gate_w, "fsdp", axis=0, tiled=True),
    )
    (
        w_in_full,
        w_out_full,
        conv_full,
        bias_full,
        a_log_full,
        dt_bias_full,
        skip_full,
        norm_full,
        gate_full,
    ) = gathered
    inputs = tokens[0].astype(jnp.float32)
    length = inputs.shape[0]
    norm_gain = norm_full.astype(jnp.float32)
    scale_in = lax.rsqrt(jnp.mean(inputs * inputs, axis=-1, keepdims=True) + EPSILON)
    normed = (inputs * scale_in * norm_gain).astype(jnp.bfloat16)
    projected = jnp.dot(normed, w_in_full, preferred_element_type=jnp.float32).astype(jnp.bfloat16)
    gate_z = projected[:, :DI].astype(jnp.float32)
    conv_in = projected[:, DI : DI + CHAN]
    dt_raw = projected[:, DI + CHAN :].astype(jnp.float32)
    first_row = lax.axis_index("seq") * length
    id_row = jnp.concatenate([jnp.full((CONV - 1,), -1, jnp.int32), segment_ids[0]], axis=0)
    ids_pad = lax.dynamic_slice_in_dim(id_row, first_row, length + CONV - 1)
    ids_own = ids_pad[CONV - 1 :]
    left_edge = passed_along(conv_in[length - (CONV - 1) :], "seq", 1)
    padded = jnp.concatenate([left_edge, conv_in], axis=0).astype(jnp.float32)
    kernel = conv_full.astype(jnp.float32)
    conv_out = jnp.zeros((length, CHAN), jnp.float32) + bias_full.astype(jnp.float32)
    same_docs = []
    for offset in range(CONV):
        same_doc = (ids_pad[offset : offset + length] == ids_own).astype(jnp.float32)
        same_docs.append(same_doc)
        conv_out = conv_out + kernel[offset] * padded[offset : offset + length] * same_doc[:, None]
    activated = jax.nn.silu(conv_out)
    blocks = length // SPAN
    x_heads = activated[:, :DI].reshape(blocks, SPAN, HEADS, HEADDIM)
    b_rows = activated[:, DI : DI + STATE].reshape(blocks, SPAN, STATE)
    c_rows = activated[:, DI + STATE :].reshape(blocks, SPAN, STATE)
    dt_bias_f = dt_bias_full.astype(jnp.float32)
    decay_rate = jnp.exp(a_log_full.astype(jnp.float32))
    step_flat = jax.nn.softplus(dt_raw + dt_bias_f)
    step_size = step_flat.reshape(blocks, SPAN, HEADS)
    log_decay = (-step_flat * decay_rate).reshape(blocks, SPAN, HEADS)
    ids_blocks = ids_own.reshape(blocks, SPAN)
    before_ids = ids_pad[CONV - 2 : CONV - 2 + length : SPAN]
    causal_mask, keep_flag, same_last = block_masks(ids_blocks, before_ids)

    def state_part(heads_in, rows_b, steps_in, decay_in):
        return local_states(heads_in, rows_b, steps_in, decay_in, same_last, keep_flag)

    (fresh_state, passing, total_state, total_decay), state_pull = jax.vjp(
        state_part, x_heads, b_rows, step_size, log_decay
    )

    def pass_forward(turn_index, received):
        return passed_along(
            (total_state + total_decay[:, None, None] * received).astype(jnp.bfloat16), "seq", 1
        ).astype(jnp.float32)

    incoming = lax.fori_loop(0, lax.axis_size("seq") - 1, pass_forward, jnp.zeros_like(total_state))

    def output_part(
        heads_in, rows_b, rows_c, steps_in, decay_in, fresh_in, passing_in, incoming_in
    ):
        return local_output(
            heads_in, rows_b, rows_c, steps_in, decay_in, incoming_in, causal_mask, keep_flag
        )

    ssd_out, output_pull = jax.vjp(
        output_part, x_heads, b_rows, c_rows, step_size, log_decay, fresh_state, passing, incoming
    )
    skip_heads = skip_full.astype(jnp.float32)
    y_full = (ssd_out + skip_heads[:, None] * x_heads).reshape(length, DI)
    silu_z = jax.nn.silu(gate_z)
    gated = y_full * silu_z
    scale_out = lax.rsqrt(jnp.mean(gated * gated, axis=-1, keepdims=True) + EPSILON)
    gate_gain = gate_full.astype(jnp.float32)
    normed_out = (gated * scale_out * gate_gain).astype(jnp.bfloat16)
    branch = jnp.dot(normed_out, w_out_full, preferred_element_type=jnp.float32)
    layer_out = (inputs + branch).astype(jnp.bfloat16)[None]
    grad_out = cotangent[0]
    d_w_out = lax.dot_general(
        normed_out, grad_out, (((0,), (0,)), ((), ())), preferred_element_type=jnp.float32
    )
    d_normed_out = lax.dot_general(
        grad_out, w_out_full, (((1,), (1,)), ((), ())), preferred_element_type=jnp.float32
    )
    d_gate_w = jnp.sum(d_normed_out * gated * scale_out, axis=0)
    along_out = d_normed_out * gate_gain
    cube_out = scale_out * scale_out * scale_out
    d_gated = scale_out * along_out - gated * cube_out * jnp.mean(
        along_out * gated, axis=-1, keepdims=True
    )
    d_y = d_gated * silu_z
    sig_z = jax.nn.sigmoid(gate_z)
    d_gate_z = d_gated * y_full * sig_z * (1.0 + gate_z * (1.0 - sig_z))
    d_ssd = d_y.reshape(blocks, SPAN, HEADS, HEADDIM)
    d_skip_grad = jnp.sum(d_ssd * x_heads, axis=(0, 1, 3))
    dx_out, db_out, dc_out, dstep_out, ddecay_out, d_fresh, d_passing, d_incoming = output_pull(
        d_ssd
    )

    def pass_backward(turn_index, received):
        return passed_along(d_incoming + total_decay[:, None, None] * received, "seq", -1)

    d_total = lax.fori_loop(0, lax.axis_size("seq") - 1, pass_backward, jnp.zeros_like(d_incoming))
    d_total_decay = jnp.sum(d_total * incoming, axis=(1, 2))
    dx_state, db_state, dstep_state, ddecay_state = state_pull(
        (d_fresh, d_passing, d_total, d_total_decay)
    )
    d_x = dx_out + dx_state + skip_heads[:, None] * d_ssd
    d_b = db_out + db_state
    d_log = (ddecay_out + ddecay_state).reshape(length, HEADS)
    d_step = (dstep_out + dstep_state).reshape(length, HEADS) - d_log * decay_rate
    d_a_log = -jnp.sum(d_log * step_flat, axis=0) * decay_rate
    d_dt_raw = d_step * jax.nn.sigmoid(dt_raw + dt_bias_f)
    d_dt_bias = jnp.sum(d_dt_raw, axis=0)
    d_act = jnp.concatenate(
        [d_x.reshape(length, DI), d_b.reshape(length, STATE), dc_out.reshape(length, STATE)], axis=1
    )
    sig_conv = jax.nn.sigmoid(conv_out)
    d_conv = d_act * sig_conv * (1.0 + conv_out * (1.0 - sig_conv))
    d_conv_b = jnp.sum(d_conv, axis=0)
    kernel_rows = []
    d_padded = jnp.zeros((length + CONV - 1, CHAN), jnp.float32)
    for offset in range(CONV):
        masked = d_conv * same_docs[offset][:, None]
        kernel_rows.append(jnp.sum(masked * padded[offset : offset + length], axis=0))
        d_padded = d_padded + jnp.pad(
            kernel[offset] * masked, ((offset, CONV - 1 - offset), (0, 0))
        )
    d_kernel = jnp.stack(kernel_rows)
    d_edge = passed_along(shortened(d_padded[: CONV - 1]), "seq", -1)
    d_conv_in = d_padded[CONV - 1 :] + jnp.pad(d_edge, ((length - (CONV - 1), 0), (0, 0)))
    d_projected = jnp.concatenate([d_gate_z, d_conv_in, d_dt_raw], axis=1).astype(jnp.bfloat16)
    d_normed = lax.dot_general(
        d_projected, w_in_full, (((1,), (1,)), ((), ())), preferred_element_type=jnp.float32
    )
    d_norm_w = jnp.sum(d_normed * inputs * scale_in, axis=0)
    along_in = d_normed * norm_gain
    cube_in = scale_in * scale_in * scale_in
    d_inputs = (
        scale_in * along_in
        - inputs * cube_in * jnp.mean(along_in * inputs, axis=-1, keepdims=True)
        + grad_out.astype(jnp.float32)
    )
    d_w_in = lax.dot_general(
        normed, d_projected, (((0,), (0,)), ((), ())), preferred_element_type=jnp.float32
    )
    weight_grads = (
        d_w_in,
        d_w_out,
        d_kernel,
        d_conv_b,
        d_a_log,
        d_dt_bias,
        d_skip_grad,
        d_norm_w,
        d_gate_w,
    )
    shares = tuple(
        (
            lax.psum_scatter(weight_grads[0], "fsdp", scatter_dimension=0, tiled=True),
            lax.psum_scatter(weight_grads[1], "fsdp", scatter_dimension=0, tiled=True),
            lax.psum_scatter(weight_grads[2], "fsdp", scatter_dimension=1, tiled=True),
            lax.psum_scatter(weight_grads[3], "fsdp", scatter_dimension=0, tiled=True),
            lax.psum_scatter(weight_grads[4], "fsdp", scatter_dimension=0, tiled=True),
            lax.psum_scatter(weight_grads[5], "fsdp", scatter_dimension=0, tiled=True),
            lax.psum_scatter(weight_grads[6], "fsdp", scatter_dimension=0, tiled=True),
            lax.psum_scatter(weight_grads[7], "fsdp", scatter_dimension=0, tiled=True),
            lax.psum_scatter(weight_grads[8], "fsdp", scatter_dimension=0, tiled=True),
        )
    )
    totals = lax.psum(shares, "seq")
    return (layer_out, d_inputs[None]) + tuple(totals)


def solution(mesh):
    return jax.shard_map(
        on_device,
        mesh=mesh,
        in_specs=(
            P("fsdp", "seq", None),
            P("fsdp", None),
            P("fsdp", "seq", None),
            P("fsdp", None),
            P("fsdp", None),
            P(None, "fsdp"),
            P("fsdp"),
            P("fsdp"),
            P("fsdp"),
            P("fsdp"),
            P("fsdp"),
            P("fsdp"),
        ),
        out_specs=(
            P("fsdp", "seq", None),
            P("fsdp", "seq", None),
            P("fsdp", None),
            P("fsdp", None),
            P(None, "fsdp"),
            P("fsdp"),
            P("fsdp"),
            P("fsdp"),
            P("fsdp"),
            P("fsdp"),
            P("fsdp"),
        ),
        check_vma=False,
    )
```

profile of v0, /device:TPU:0, one launch (start us, length us, event | category | flops | bytes accessed | tf_op | source)
XLA Modules:
  0.0 1851.0 jit_solution(16285410717219535761)
XLA Ops:
  9.6 13.5 all-gather.1
  23.2 13.2 all-gather
  40.1 30.4 %all-reduce.20 = (bf16[3328]{0:T(1024)(128)(2,1)S(1)}, bf16[48]{0:T(256)(128)(2,1)S(1)}, bf16[48]{0:T(256)(128)(2,1)S(1)}, bf16[48]{0:T(256)(128)(2,1)S(1)}) all-reduce(bf16[3328]{0:T(1024)(128)(2,1)S(1)} %dynamic-update-slice, bf16[48]{0:T(256)(128)(2,1)S(1)} %dynamic-update-slice.2, ...), channel_id=1, replica_groups=mesh['seq'=8,'fsdp'=4] {'fsdp'}, use_global_device_ids=true, to_apply=%add.7 | all-reduce | flops 3472 | bytes 13888
  74.6 30.3 %all-gather.2 = bf16[4,1,768]{2,1,0:T(2,128)(2,1)S(1)} all-gather(bf16[1,1,768]{2,1,0:T(2,128)(2,1)S(1)} %reshape.689), channel_id=1, replica_groups=mesh['seq'=8,'fsdp'=4] {'fsdp'}, dimensions={0}, use_global_device_ids=true | all-gather | bytes 7680 | tf_op jit(solution)/shard_map/all_gather | solution.py:94
  107.8 243.6 %all-gather.6.cloned.1.call-done = bf16[1536,6448]{0,1:T(8,128)(2,1)} async-done(((bf16[384,6448]{0,1:T(8,128)(2,1)}), bf16[1536,6448]{0,1:T(8,128)(2,1)}) %all-gather.6.cloned.1.call-update) | async-done | bytes 19808272 | tf_op jit(solution)/shard_map/all_gather | solution.py:86
  351.4 9.9 convolution_convert_fusion
  385.7 4.7 fusion.27
  394.2 3.6 copy.162
  399.8 5.7 fusion.61
  405.6 122.4 %while.22 = (s32[]{:T(128)}, f32[48,64,128]{2,1,0:T(8,128)}, f32[1,48]{1,0:T(1,128)}, f32[48,64,128]{2,1,0:T(8,128)}, s32[]{:T(128)}, /*index=5*/s32[]{:T(128)}) while((s32[]{:T(128)}, f32[48,64,128]{2,1,0:T(8,128)}, f32[1,48]{1,0:T(1,128)}, f32[48,64,128]{2,1,0:T(8,128)}, s32[]{:T(128)}, /*index=5*/s32[]{:T(128)}) %tuple.82), condition=%wide.region_4.5_spmd.clone, body=%wide.region_3.4_spmd.clone.sunk | while | flops 1966083 | bytes 9437495 | solution.py:155
  408.1 3.9 collective-permute-start.1
  418.9 9.9 collective-permute-start.1
  432.5 3.0 fusion.137
  435.6 12.3 collective-permute-start.1
  454.6 12.3 collective-permute-start.1
  473.8 12.3 collective-permute-start.1
  492.8 12.3 collective-permute-start.1
  511.9 12.3 collective-permute-start.1
  528.1 4.2 fusion.94
  532.4 16.3 fusion.35
  548.7 3.5 copy.171
  552.2 3.6 multiply_reduce_fusion.10
  557.5 8.0 fusion.76
  568.2 3.8 copy.174
  572.0 8.4 multiply_reduce_fusion.6
  580.4 5.6 multiply_reduce_fusion.7
  586.1 3.9 copy.173
  590.0 5.0 mul.702
  595.0 3.6 copy.175
  598.6 5.6 fusion.92
  605.6 173.4 %while.21 = (s32[]{:T(128)}, f32[48,64,128]{2,1,0:T(8,128)}, f32[1,48]{1,0:T(1,128)}, f32[48,64,128]{2,1,0:T(8,128)}, s32[]{:T(128)}) while((s32[]{:T(128)}, f32[48,64,128]{2,1,0:T(8,128)}, f32[1,48]{1,0:T(1,128)}, f32[48,64,128]{2,1,0:T(8,128)}, s32[]{:T(128)}) %tuple.102), condition=%wide.region_8.9_spmd, body=%wide.region_7.8_spmd.sunk | while | flops 786434 | bytes 11010341 | solution.py:201
  605.6 3.3 multiply_add_fusion.4
  610.2 13.1 collective-permute-done
  623.3 3.3 multiply_add_fusion.4
  628.0 22.6 %collective-permute-done = f32[48,64,128]{2,1,0:T(8,128)} collective-permute-done((f32[48,64,128]{2,1,0:T(8,128)}, f32[48,64,128]{2,1,0:T(8,128)}, u32[]{:S(2)}, u32[]{:S(2)}) %collective-permute-start) | collective-permute-done | bytes 1572896 | tf_op jit(solution)/shard_map/while/body/eval_jaxpr/ppermute | solution.py:20
  650.6 3.3 multiply_add_fusion.4
  655.2 21.0 %collective-permute-done = f32[48,64,128]{2,1,0:T(8,128)} collective-permute-done((f32[48,64,128]{2,1,0:T(8,128)}, f32[48,64,128]{2,1,0:T(8,128)}, u32[]{:S(2)}, u32[]{:S(2)}) %collective-permute-start) | collective-permute-done | bytes 1572896 | tf_op jit(solution)/shard_map/while/body/eval_jaxpr/ppermute | solution.py:20
  676.2 3.3 multiply_add_fusion.4
  680.8 21.1 %collective-permute-done = f32[48,64,128]{2,1,0:T(8,128)} collective-permute-done((f32[48,64,128]{2,1,0:T(8,128)}, f32[48,64,128]{2,1,0:T(8,128)}, u32[]{:S(2)}, u32[]{:S(2)}) %collective-permute-start) | collective-permute-done | bytes 1572896 | tf_op jit(solution)/shard_map/while/body/eval_jaxpr/ppermute | solution.py:20
  701.9 3.3 multiply_add_fusion.4
  706.5 21.0 %collective-permute-done = f32[48,64,128]{2,1,0:T(8,128)} collective-permute-done((f32[48,64,128]{2,1,0:T(8,128)}, f32[48,64,128]{2,1,0:T(8,128)}, u32[]{:S(2)}, u32[]{:S(2)}) %collective-permute-start) | collective-permute-done | bytes 1572896 | tf_op jit(solution)/shard_map/while/body/eval_jaxpr/ppermute | solution.py:20
  727.6 3.6 multiply_add_fusion.4
  732.4 20.8 %collective-permute-done = f32[48,64,128]{2,1,0:T(8,128)} collective-permute-done((f32[48,64,128]{2,1,0:T(8,128)}, f32[48,64,128]{2,1,0:T(8,128)}, u32[]{:S(2)}, u32[]{:S(2)}) %collective-permute-start) | collective-permute-done | bytes 1572896 | tf_op jit(solution)/shard_map/while/body/eval_jaxpr/ppermute | solution.py:20
  753.2 3.4 multiply_add_fusion.4
  758.0 21.0 %collective-permute-done = f32[48,64,128]{2,1,0:T(8,128)} collective-permute-done((f32[48,64,128]{2,1,0:T(8,128)}, f32[48,64,128]{2,1,0:T(8,128)}, u32[]{:S(2)}, u32[]{:S(2)}) %collective-permute-start) | collective-permute-done | bytes 1572896 | tf_op jit(solution)/shard_map/while/body/eval_jaxpr/ppermute | solution.py:20
  779.0 7.4 fusion.37
  787.9 23.3 %fusion.10 = (f32[48,256]{1,0:T(8,128)}, f32[48,256]{1,0:T(8,128)}, f32[48,256]{1,0:T(8,128)}, f32[256,256]{1,0:T(8,128)}) fusion(f32[48,256]{1,0:T(8,128)} %copy.166, f32[256,256]{1,0:T(8,128)} %get-tuple-element.160, f32[48,256]{1,0:T(8,128)} %bitcast_add_fusion.7, f32[256,256]{1,0:T(8,128)} %fusion.101, pred[256,256]{1,0:T(8,128)(4,1)} %get-tuple-element.159, ...), kind=kOutput, calls=%fused_computation.15 | convolution fusion | flops 2463002624 | bytes 7389184 | tf_op jit(solution)/shard_map/transpose(jvp(chts,cshp->cthp))/dot_general | solution.py:63
  814.3 4.2 multiply_reduce_fusion.8
  827.2 3.8 reduce-window.26
  835.4 3.8 reduce-window.24
  841.8 15.3 fusion.34
  857.2 3.7 copy.180
  862.6 7.5 convolution_bitcast_fusion
  871.7 6.5 fusion.72
  878.3 4.8 multiply_reduce_fusion.5
  895.1 11.3 collective-permute-done.3
  908.6 17.6 fusion.64
  928.9 661.6 %reduce-scatter.6.cloned.1.call-done = f32[384,6448]{0,1:T(8,128)} async-done(((f32[1536,6448]{0,1:T(8,128)}), f32[384,6448]{0,1:T(8,128)}) %reduce-scatter.6.cloned.1.call-update) | async-done | bytes 9904144 | tf_op jit(solution)/shard_map/reduce_scatter | solution.py:258
  1593.8 7.5 fusion.43
  1601.4 9.9 fusion.57
  1611.4 22.4 %all-reduce.19 = (f32[3328]{0:T(1024)S(1)}, f32[48]{0:T(128)S(1)}, f32[48]{0:T(128)S(1)}, f32[48]{0:T(128)S(1)}, f32[1536]{0:T(1024)S(1)}, /*index=5*/f32[3072]{0:T(1024)S(1)}) all-reduce(f32[3328]{0:T(1024)S(1)} %copy-done.36, f32[48]{0:T(128)S(1)} %negate_multiply_fusion.1, ...), channel_id=5, replica_groups=mesh['seq'=8,'fsdp'=4] {'fsdp'}, use_global_device_ids=true, to_apply=%region_33.34.clone | all-reduce | flops 8080 | bytes 64640
  1637.0 24.0 %all-reduce.17 = (f32[4,832]{1,0:T(4,128)}, f32[832]{0:T(1024)}, f32[12]{0:T(128)}, f32[12]{0:T(128)}, f32[12]{0:T(128)}, /*index=5*/f32[384]{0:T(512)}, f32[768]{0:T(1024)}) all-reduce(f32[4,832]{1,0:T(4,128)S(1)} %copy.204, f32[832]{0:T(1024)S(1)} %dynamic-slice.5, ...), channel_id=1, replica_groups=mesh['seq'=8,'fsdp'=4] {'seq'}, use_global_device_ids=true, to_apply=%region_31.32 | all-reduce | flops 5348 | bytes 42784 | tf_op jit(solution)/shard_map/psum | solution.py:269
  1661.0 172.3 %all-reduce.23.cloned.1.call-done = (f32[384,6448]{0,1:T(8,128)}, f32[768,1536]{1,0:T(8,128)}) async-done(((f32[384,6448]{0,1:T(8,128)}, f32[768,1536]{1,0:T(8,128)}), (f32[384,6448]{0,1:T(8,128)}, f32[768,1536]{1,0:T(8,128)})) %all-reduce.23.cloned.1.call-update) | async-done | bytes 14622736 | tf_op jit(solution)/shard_map/psum | solution.py:269
  1833.2 8.5 copy.227
  (311 shorter events, 146.7 us)
Async XLA Ops:
  7.2 29.9 %copy-start.69 = (u32[32]{0:T(128)S(1)}, u32[32]{0:T(128)}, u32[]{:S(2)}) copy-start(u32[32]{0:T(128)} %constant.79) | copy-start | bytes 388
  7.2 15.9 copy-start.64
  7.2 31.8 %copy-start.76 = (bf16[12]{0:T(256)(128)(2,1)S(1)}, bf16[12]{0:T(256)(128)(2,1)}, u32[]{:S(2)}) copy-start(bf16[12]{0:T(256)(128)(2,1)} %param.23) | copy-start | bytes 76
  7.2 32.1 %copy-start.77 = (bf16[12]{0:T(256)(128)(2,1)S(1)}, bf16[12]{0:T(256)(128)(2,1)}, u32[]{:S(2)}) copy-start(bf16[12]{0:T(256)(128)(2,1)} %param.24) | copy-start | bytes 76
  7.2 32.3 %copy-start.78 = (bf16[12]{0:T(256)(128)(2,1)S(1)}, bf16[12]{0:T(256)(128)(2,1)}, u32[]{:S(2)}) copy-start(bf16[12]{0:T(256)(128)(2,1)} %param.25) | copy-start | bytes 76
  7.3 32.6 %copy-start.70 = (bf16[832]{0:T(1024)(128)(2,1)S(1)}, bf16[832]{0:T(1024)(128)(2,1)}, u32[]{:S(2)}) copy-start(bf16[832]{0:T(1024)(128)(2,1)} %param.22) | copy-start | bytes 4996
  7.3 67.3 %copy-start.71 = (bf16[768]{0:T(1024)(128)(2,1)S(1)}, bf16[768]{0:T(1024)(128)(2,1)}, u32[]{:S(2)}) copy-start(bf16[768]{0:T(1024)(128)(2,1)} %param.27) | copy-start | bytes 4612
  7.3 98.3 %copy-start.12 = (bf16[1,256,1536]{2,1,0:T(8,128)(2,1)S(1)}, bf16[1,256,1536]{2,1,0:T(8,128)(2,1)}, u32[]{:S(2)}) copy-start(bf16[1,256,1536]{2,1,0:T(8,128)(2,1)} %param.16) | copy-start | bytes 2359300
  7.3 344.1 %all-gather.6.cloned.1.call-start = ((), (), s32[]{:S(2)}) async-start(), calls=%async_computation.3 | async-start | bytes 24760320 | tf_op jit(solution)/shard_map/all_gather | solution.py:86
  8.0 564.0 %all-gather.8.cloned.1.call-start = ((), (), s32[]{:S(2)}) async-start(), calls=%async_computation.4 | async-start | bytes 11796480 | tf_op jit(solution)/shard_map/all_gather | solution.py:87
  8.8 920.1 %reduce-scatter.8.cloned.1.call-start = ((), (), s32[]{:S(2)}) async-start(), calls=%async_computation.6 | async-start | bytes 23592960 | tf_op jit(solution)/shard_map/reduce_scatter | solution.py:259
  70.4 281.0 %copy-start.79 = (bf16[48]{0:T(256)(128)(2,1)}, bf16[48]{0:T(256)(128)(2,1)S(1)}, u32[]{:S(2)}) copy-start(bf16[48]{0:T(256)(128)(2,1)S(1)} %get-tuple-element.123) | copy-start | bytes 292
  73.5 301.8 %copy-start.47 = (f32[256]{0:T(256)}, f32[256]{0:T(256)S(1)}, u32[]{:S(2)}) copy-start(f32[256]{0:T(256)S(1)} %get-tuple-element.150) | copy-start | bytes 3076
  351.4 10.0 copy-start.58
  351.4 10.0 copy-start.72
  351.4 17.2 copy-start.55
  361.3 22.6 %copy-start.11 = (bf16[256,6448]{1,0:T(8,128)(2,1)}, bf16[256,6448]{1,0:T(8,128)(2,1)S(1)}, u32[]{:S(2)}) copy-start(bf16[256,6448]{1,0:T(8,128)(2,1)S(1)} %convolution_convert_fusion) | copy-start | bytes 9904132
  365.8 18.1 collective-permute-start.2
  370.3 13.6 copy-start.20
  373.8 10.1 copy-start.61
  408.1 5.3 collective-permute-start.1
  418.9 11.2 collective-permute-start.1
  435.6 13.6 collective-permute-start.1
  454.6 13.7 collective-permute-start.1
  473.8 13.6 collective-permute-start.1
  492.8 13.6 collective-permute-start.1
  511.9 13.6 collective-permute-start.1
  532.3 16.4 copy-start.9
  565.5 1025.0 %reduce-scatter.6.cloned.1.call-start = ((), (), s32[]{:S(2)}) async-start(), calls=%async_computation.5 | async-start | bytes 49520640 | tf_op jit(solution)/shard_map/reduce_scatter | solution.py:258
  572.0 8.4 copy-start.3
  572.0 8.4 copy-start.5
  572.0 8.4 copy-start.7
  572.0 8.4 copy-start.51
  572.0 8.4 copy-start.68
  608.9 14.4 collective-permute-start
  626.7 23.9 %collective-permute-start = (f32[48,64,128]{2,1,0:T(8,128)}, f32[48,64,128]{2,1,0:T(8,128)}, u32[]{:S(2)}, u32[]{:S(2)}) collective-permute-start(f32[48,64,128]{2,1,0:T(8,128)} %multiply_add_fusion.4), channel_id=1, source_target_pairs={{4,0},{8,4},{12,8},{16,12},{20,16},{24,20},{28,24},{5,1},{9,5},{13... | collective-permute-start | bytes 4718600 | tf_op jit(solution)/shard_map/while/body/eval_jaxpr/ppermute | solution.py:20
  653.9 22.3 %collective-permute-start = (f32[48,64,128]{2,1,0:T(8,128)}, f32[48,64,128]{2,1,0:T(8,128)}, u32[]{:S(2)}, u32[]{:S(2)}) collective-permute-start(f32[48,64,128]{2,1,0:T(8,128)} %multiply_add_fusion.4), channel_id=1, source_target_pairs={{4,0},{8,4},{12,8},{16,12},{20,16},{24,20},{28,24},{5,1},{9,5},{13... | collective-permute-start | bytes 4718600 | tf_op jit(solution)/shard_map/while/body/eval_jaxpr/ppermute | solution.py:20
  679.5 22.4 %collective-permute-start = (f32[48,64,128]{2,1,0:T(8,128)}, f32[48,64,128]{2,1,0:T(8,128)}, u32[]{:S(2)}, u32[]{:S(2)}) collective-permute-start(f32[48,64,128]{2,1,0:T(8,128)} %multiply_add_fusion.4), channel_id=1, source_target_pairs={{4,0},{8,4},{12,8},{16,12},{20,16},{24,20},{28,24},{5,1},{9,5},{13... | collective-permute-start | bytes 4718600 | tf_op jit(solution)/shard_map/while/body/eval_jaxpr/ppermute | solution.py:20
  705.2 22.3 %collective-permute-start = (f32[48,64,128]{2,1,0:T(8,128)}, f32[48,64,128]{2,1,0:T(8,128)}, u32[]{:S(2)}, u32[]{:S(2)}) collective-permute-start(f32[48,64,128]{2,1,0:T(8,128)} %multiply_add_fusion.4), channel_id=1, source_target_pairs={{4,0},{8,4},{12,8},{16,12},{20,16},{24,20},{28,24},{5,1},{9,5},{13... | collective-permute-start | bytes 4718600 | tf_op jit(solution)/shard_map/while/body/eval_jaxpr/ppermute | solution.py:20
  731.1 22.1 %collective-permute-start = (f32[48,64,128]{2,1,0:T(8,128)}, f32[48,64,128]{2,1,0:T(8,128)}, u32[]{:S(2)}, u32[]{:S(2)}) collective-permute-start(f32[48,64,128]{2,1,0:T(8,128)} %multiply_add_fusion.4), channel_id=1, source_target_pairs={{4,0},{8,4},{12,8},{16,12},{20,16},{24,20},{28,24},{5,1},{9,5},{13... | collective-permute-start | bytes 4718600 | tf_op jit(solution)/shard_map/while/body/eval_jaxpr/ppermute | solution.py:20
  756.7 22.3 %collective-permute-start = (f32[48,64,128]{2,1,0:T(8,128)}, f32[48,64,128]{2,1,0:T(8,128)}, u32[]{:S(2)}, u32[]{:S(2)}) collective-permute-start(f32[48,64,128]{2,1,0:T(8,128)} %multiply_add_fusion.4), channel_id=1, source_target_pairs={{4,0},{8,4},{12,8},{16,12},{20,16},{24,20},{28,24},{5,1},{9,5},{13... | collective-permute-start | bytes 4718600 | tf_op jit(solution)/shard_map/while/body/eval_jaxpr/ppermute | solution.py:20
  860.9 9.3 copy-start.23
  860.9 10.8 copy-start.1
  860.9 10.8 copy-start.27
  862.6 15.6 copy-start.10
  870.2 8.0 copy-start.8
  870.2 8.0 copy-start.44
  870.2 8.0 copy-start.45
  870.2 8.0 copy-start.46
  884.3 8.2 copy-start.49
  884.3 8.2 copy-start.60
  884.3 8.2 copy-start.63
  886.0 20.4 %collective-permute-start.3 = (bf16[3,3328]{1,0:T(4,128)(2,1)}, bf16[3,3328]{1,0:T(4,128)(2,1)}, u32[]{:S(2)}, u32[]{:S(2)}) collective-permute-start(bf16[3,3328]{1,0:T(4,128)(2,1)} %slice.240), channel_id=1, source_target_pairs={{4,0},{8,4},{12,8},{16,12},{20,16},{24,20},{28,24},{5,1},{9,5},{13... | collective-permute-start | bytes 59912 | tf_op jit(solution)/shard_map/ppermute | solution.py:20
  926.2 709.6 %reduce-scatter.10.cloned.1.call-start = ((), (), s32[]{:S(2)}) async-start(), calls=%async_computation.7 | async-start | bytes 2129920
  928.8 904.4 %all-reduce.23.cloned.1.call-start = ((), (), s32[]{:S(2)}) async-start(), calls=%async_computation.8 | async-start | bytes 29245440 | tf_op jit(solution)/shard_map/psum | solution.py:269
  1593.8 7.5 copy-start.13
  1593.8 7.5 copy-start.15
  1601.4 10.0 copy-start.36
  1601.4 10.0 copy-start.53
  1601.4 10.0 copy-start.73
  1601.4 32.8 %copy-start.14 = (bf16[1,256,1536]{2,1,0:T(8,128)(2,1)S(1)}, bf16[1,256,1536]{2,1,0:T(8,128)(2,1)}, u32[]{:S(2)}) copy-start(bf16[1,256,1536]{2,1,0:T(8,128)(2,1)} %param.16) | copy-start | bytes 2359300
  1601.4 32.8 %copy-start.19 = (bf16[1,256,1536]{2,1,0:T(8,128)(2,1)S(1)}, bf16[1,256,1536]{2,1,0:T(8,128)(2,1)}, u32[]{:S(2)}) copy-start(bf16[1,256,1536]{2,1,0:T(8,128)(2,1)} %param.18) | copy-start | bytes 2359300
  1601.4 32.8 %copy-start.67 = (f32[256]{0:T(256)S(1)}, f32[256]{0:T(256)}, u32[]{:S(2)}) copy-start(f32[256]{0:T(256)} %get-tuple-element.155) | copy-start | bytes 3076
  1833.2 8.5 copy-start.17
  (40 other events, 125.9 us)
Sparse Core Ops, SparseCore 0:
  9.7 341.6 all-gather.5
  353.0 165.5 all-gather.7
  565.6 328.2 reduce-scatter.7
  926.4 664.1 reduce-scatter.5
  1593.4 40.8 reduce-scatter.9
  1638.4 194.8 all-reduce.22
where the time goes:
time: 1860 us; the launch traced here: 1850 us
  waiting for transfers between devices  1240 us (67%)
  matrix products  158 us (8%)
  blocking collectives  134 us (7%)
  other arithmetic  131 us (7%)
  starting transfers between devices  88.3 us (5%)
  local copies, waits for them, and re-layouts  79.2 us (4%)
  between operations  19.7 us (1%)
    reduce_scatter x1, waiting for transfers between devices, on_device(): lax.psum_scatter(weight_grads[0], 'fsdp', scatter_dimension=0, tiled=True)  662 us
    all_gather x1, waiting for transfers between devices, on_device(): lax.all_gather(w_in, 'fsdp', axis=0, tiled=True)  244 us
    psum x1, waiting for transfers between devices, on_device(): totals = lax.psum(shares, 'seq')  172 us
    ppermute x16, waiting for transfers between devices, passed_along(): lax.ppermute(value, axis, [(source, source + steps) for source in range(f...  161 us
    ppermute x16, starting transfers between devices, passed_along(): lax.ppermute(value, axis, [(source, source + steps) for source in range(f...  88.1 us
    dot_general x3, matrix products, local_output(): jnp.einsum('chts,cshp->cthp', mixing, x_heads, precision=HIGHEST)  54.9 us
    unnamed x2, blocking collectives  52.7 us
  transfers between devices with their start and end apart: 22, of which 18 were waited for; matrix products, arithmetic and copies ran while one was open for 19% of the time, Pallas kernels for 0%

commit v1 on v0

--- a/solution.py
+++ b/solution.py
@@ -1,3 +1,4 @@
+import functools
 import jax
 import jax.numpy as jnp
 from jax import lax
@@ -12,6 +13,32 @@
 CHAN = 3328
 EPSILON = 1e-05
 HIGHEST = lax.Precision.HIGHEST
+
+
+def _make_pools(vec, k_dim):
+    piece_next = list(vec.shape[1:])
+    piece_next[k_dim] *= vec.shape[0]
+    shaped = jnp.moveaxis(vec, 0, k_dim).reshape(piece_next)
+    return shaped
+
+
+def start_the_rails(message, row_axis):
+    e_now, now = (jax.lax.axis_size(row_axis), jax.lax.axis_index(row_axis))
+    opened, lower = (message[None], 1)
+    while lower < e_now:
+        known = jax.lax.ppermute(opened, row_axis, [(q, q ^ lower) for q in range(e_now)])
+        val = now & lower == 0
+        opened = jnp.concatenate([jnp.where(val, opened, known), jnp.where(val, known, opened)])
+        lower *= 2
+    return opened
+
+
+def trace_the_modes(local_block, mat, array_dim):
+    piece_now = _make_pools(start_the_rails(local_block, mat), array_dim)
+    return piece_now
+
+
+step_on_layers_all_now = functools.partial(trace_the_modes, mat="fsdp", array_dim=0)
 
 
 def passed_along(value, axis, steps):
@@ -83,7 +110,7 @@
     gate_w,
 ):
     gathered = (
-        lax.all_gather(w_in, "fsdp", axis=0, tiled=True),
+        step_on_layers_all_now(w_in),
         lax.all_gather(w_out, "fsdp", axis=0, tiled=True),
         lax.all_gather(conv_w, "fsdp", axis=1, tiled=True),
         lax.all_gather(conv_b, "fsdp", axis=0, tiled=True),

time: 1860 us -> 2320 us (1.25)
  blocking collectives: 134 us -> 664 us
  waiting for transfers between devices: 1240 us -> 1100 us
  other arithmetic: 131 us -> 166 us
  local copies, waits for them, and re-layouts: 79.2 us -> 105 us
    all_gather x1, blocking collectives: 13.5 us -> 583 us  [on_device(): lax.all_gather(norm_w, 'fsdp', axis=0, tiled=True)]
    all_gather x1 -> x0, waiting for transfers between devices: 244 us -> none  [on_device(): lax.all_gather(w_in, 'fsdp', axis=0, tiled=True)]
    ppermute x0 -> x2, waiting for transfers between devices: none -> 107 us  [start_the_rails(): jax.lax.ppermute(opened, row_axis, [(q, q ^ lower) for q in range(e_now)])]
    concatenate x0 -> x1, local copies, waits for them, and re-layouts: none -> 25.3 us  [start_the_rails(): jnp.concatenate([jnp.where(val, opened, known), jnp.where(val, known, ope...]
  transfers between devices with their start and end apart: 22 -> 23, of which waited for: 18 -> 18; matrix products, arithmetic and copies ran while one was open for 19% -> 17% of each run, Pallas kernels for 0% -> 0%
where the time goes in v1:
time: 2320 us; the launch traced here: 2310 us
  waiting for transfers between devices  1100 us (47%)
  blocking collectives  664 us (29%)
  other arithmetic  166 us (7%)
  matrix products  162 us (7%)
  local copies, waits for them, and re-layouts  105 us (5%)
  starting transfers between devices  93.8 us (4%)
    reduce_scatter x1, waiting for transfers between devices, on_device(): lax.psum_scatter(weight_grads[0], 'fsdp', scatter_dimension=0, tiled=True)  663 us
    all_gather x1, blocking collectives, on_device(): lax.all_gather(norm_w, 'fsdp', axis=0, tiled=True)  583 us
    psum x1, waiting for transfers between devices, on_device(): totals = lax.psum(shares, 'seq')  172 us
    ppermute x16, waiting for transfers between devices, passed_along(): lax.ppermute(value, axis, [(source, source + steps) for source in range(f...  161 us
    ppermute x2, waiting for transfers between devices, start_the_rails(): jax.lax.ppermute(opened, row_axis, [(q, q ^ lower) for q in range(e_now)])  107 us
    ppermute x16, starting transfers between devices, passed_along(): lax.ppermute(value, axis, [(source, source + steps) for source in range(f...  87.8 us
    dot_general x3, matrix products, local_output(): jnp.einsum('chts,cshp->cthp', mixing, x_heads, precision=HIGHEST)  54.3 us
  transfers between devices with their start and end apart: 23, of which 18 were waited for; matrix products, arithmetic and copies ran while one was open for 17% of the time, Pallas kernels for 0%

profile of v1, /device:TPU:0, one launch (start us, length us, event | category | flops | bytes accessed | tf_op | source)
XLA Modules:
  0.0 2312.2 jit_solution(12500215099880276874)
XLA Ops:
  10.3 107.1 %collective-permute-done.2 = bf16[1,384,6448]{1,2,0:T(8,128)(2,1)} collective-permute-done((bf16[1,384,6448]{1,2,0:T(8,128)(2,1)}, bf16[1,384,6448]{1,2,0:T(8,128)(2,1)}, u32[]{:S(2)}, u32[]{:S(2)}) %collective-permute-start.2) | collective-permute-done | bytes 4952096 | tf_op jit(solution)/shard_map/ppermute | solution.py:29
  117.4 8.6 broadcast_select_fusion.3
  126.1 9.0 pad_maximum_fusion.1
  138.7 582.7 %all-gather.1 = bf16[4,1,384]{2,1,0:T(2,128)(2,1)S(1)} all-gather(bf16[1,1,384]{2,1,0:T(2,128)(2,1)S(1)} %reshape.705), channel_id=1, replica_groups=mesh['seq'=8,'fsdp'=4] {'fsdp'}, dimensions={0}, use_global_device_ids=true | all-gather | bytes 3840 | tf_op jit(solution)/shard_map/all_gather | solution.py:120
  721.4 13.1 all-gather
  738.2 8.7 all-reduce.20
  751.2 13.0 all-gather.2
  767.1 8.1 broadcast_select_fusion.1
  775.2 8.5 pad_maximum_fusion
  783.7 25.3 %copy.166 = bf16[4,384,6448]{2,1,0:T(8,128)(2,1)} copy(bf16[4,384,6448]{1,2,0:T(8,128)(2,1)} %pad_maximum_fusion) | data formatting | bytes 39616512 | tf_op jit(solution)/shard_map/concatenate | solution.py:31
  809.0 12.7 convolution_convert_fusion
  845.5 4.7 fusion.27
  854.0 3.5 copy.168
  859.6 5.7 fusion.68
  865.4 122.9 %while.22 = (s32[]{:T(128)}, f32[48,64,128]{2,1,0:T(8,128)}, f32[1,48]{1,0:T(1,128)}, f32[48,64,128]{2,1,0:T(8,128)}, s32[]{:T(128)}, /*index=5*/s32[]{:T(128)}) while((s32[]{:T(128)}, f32[48,64,128]{2,1,0:T(8,128)}, f32[1,48]{1,0:T(1,128)}, f32[48,64,128]{2,1,0:T(8,128)}, s32[]{:T(128)}, /*index=5*/s32[]{:T(128)}) %tuple.84), condition=%wide.region_4.5_spmd.clone, body=%wide.region_3.4_spmd.clone.sunk | while | flops 1966083 | bytes 9437495 | solution.py:182
  867.9 4.4 collective-permute-start.1
  879.2 9.8 collective-permute-start.1
  895.8 12.3 collective-permute-start.1
  914.9 12.3 collective-permute-start.1
  934.0 12.3 collective-permute-start.1
  953.1 12.3 collective-permute-start.1
  972.2 12.3 collective-permute-start.1
  988.3 4.2 fusion.106
  992.6 16.0 fusion.35
  1008.6 3.5 copy.177
  1012.2 3.6 multiply_reduce_fusion.10
  1017.5 8.0 fusion.86
  1028.2 4.0 copy.180
  1032.2 8.4 multiply_reduce_fusion.6
  1040.7 5.6 multiply_reduce_fusion.7
  1046.3 4.1 copy.179
  1050.4 5.0 mul.713
  1055.5 3.6 copy.181
  1059.0 5.6 fusion.104
  1066.0 172.5 %while.21 = (s32[]{:T(128)}, f32[48,64,128]{2,1,0:T(8,128)}, f32[1,48]{1,0:T(1,128)}, f32[48,64,128]{2,1,0:T(8,128)}, s32[]{:T(128)}) while((s32[]{:T(128)}, f32[48,64,128]{2,1,0:T(8,128)}, f32[1,48]{1,0:T(1,128)}, f32[48,64,128]{2,1,0:T(8,128)}, s32[]{:T(128)}) %tuple.102), condition=%wide.region_8.9_spmd, body=%wide.region_7.8_spmd.sunk | while | flops 786434 | bytes 11010341 | solution.py:228
  1070.7 12.9 collective-permute-done
  1083.6 3.3 multiply_add_fusion.4
  1088.2 22.0 collective-permute-done
  1114.8 21.0 collective-permute-done
  1140.5 21.0 collective-permute-done
  1161.5 3.4 multiply_add_fusion.4
  1166.2 21.0 collective-permute-done
  1187.2 3.3 multiply_add_fusion.4
  1191.8 21.0 collective-permute-done
  1217.5 21.0 collective-permute-done
  1238.5 7.4 fusion.37
  1247.5 23.0 fusion.10
  1273.6 4.2 multiply_reduce_fusion.8
  1287.3 3.8 reduce-window.26
  1295.5 3.8 reduce-window.24
  1302.0 15.3 fusion.34
  1317.4 3.9 copy.186
  1323.1 7.5 convolution_bitcast_fusion
  1332.1 6.5 fusion.79
  1338.7 4.7 multiply_reduce_fusion.5
  1355.5 11.3 collective-permute-done.5
  1369.0 17.6 fusion.71
  1389.3 662.9 %reduce-scatter.6.cloned.1.call-done = f32[384,6448]{0,1:T(8,128)} async-done(((f32[1536,6448]{0,1:T(8,128)}), f32[384,6448]{0,1:T(8,128)}) %reduce-scatter.6.cloned.1.call-update) | async-done | bytes 9904144 | tf_op jit(solution)/shard_map/reduce_scatter | solution.py:285
  2055.3 7.4 fusion.43
  2062.7 11.1 fusion.62
  2073.9 22.1 all-reduce.19
  2099.2 24.0 %all-reduce.17 = (f32[4,832]{1,0:T(4,128)}, f32[832]{0:T(1024)}, f32[12]{0:T(128)}, f32[12]{0:T(128)}, f32[12]{0:T(128)}, /*index=5*/f32[384]{0:T(512)}, f32[768]{0:T(1024)}) all-reduce(f32[4,832]{1,0:T(4,128)S(1)} %copy.210, f32[832]{0:T(1024)S(1)} %dynamic-slice.5, ...), channel_id=1, replica_groups=mesh['seq'=8,'fsdp'=4] {'seq'}, use_global_device_ids=true, to_apply=%region_31.32 | all-reduce | flops 5348 | bytes 42784 | tf_op jit(solution)/shard_map/psum | solution.py:296
  2123.2 171.6 %all-reduce.23.cloned.1.call-done = (f32[384,6448]{0,1:T(8,128)}, f32[768,1536]{1,0:T(8,128)}) async-done(((f32[384,6448]{0,1:T(8,128)}, f32[768,1536]{1,0:T(8,128)}), (f32[384,6448]{0,1:T(8,128)}, f32[768,1536]{1,0:T(8,128)})) %all-reduce.23.cloned.1.call-update) | async-done | bytes 14622736 | tf_op jit(solution)/shard_map/psum | solution.py:296
  2294.8 8.5 copy.233
  (293 shorter events, 168.2 us)
Async XLA Ops:
  7.2 1025.0 %all-gather.5.cloned.1.call-start = ((), (), s32[]{:S(2)}) async-start(), calls=%async_computation.3 | async-start | bytes 11796480 | tf_op jit(solution)/shard_map/all_gather | solution.py:114
  7.2 110.2 %collective-permute-start.2 = (bf16[1,384,6448]{1,2,0:T(8,128)(2,1)}, bf16[1,384,6448]{1,2,0:T(8,128)(2,1)}, u32[]{:S(2)}, u32[]{:S(2)}) collective-permute-start(bf16[1,384,6448]{1,2,0:T(8,128)(2,1)} %bitcast.324), channel_id=1, source_target_pairs={{0,1},{1,0},{2,3},{3,2},{4,5},{5,4},{6,7},{7,6},{8,9},{9,8},{10,11... | collective-permute-start | bytes 14856200 | tf_op jit(solution)/shard_map/ppermute | solution.py:29
  126.1 11.9 copy-start.47
  126.1 12.6 copy-start.62
  126.1 595.4 %copy-start.52 = (bf16[4,832]{1,0:T(4,128)(2,1)S(1)}, bf16[4,832]{1,0:T(4,128)(2,1)}, u32[]{:S(2)}) copy-start(bf16[4,832]{1,0:T(4,128)(2,1)} %param.21) | copy-start | bytes 19972
  126.1 609.2 %copy-start.57 = (u32[32]{0:T(128)S(1)}, u32[32]{0:T(128)}, u32[]{:S(2)}) copy-start(u32[32]{0:T(128)} %constant.86) | copy-start | bytes 388
  126.1 611.1 %copy-start.64 = (bf16[12]{0:T(256)(128)(2,1)S(1)}, bf16[12]{0:T(256)(128)(2,1)}, u32[]{:S(2)}) copy-start(bf16[12]{0:T(256)(128)(2,1)} %param.23) | copy-start | bytes 76
  126.1 611.4 %copy-start.65 = (bf16[12]{0:T(256)(128)(2,1)S(1)}, bf16[12]{0:T(256)(128)(2,1)}, u32[]{:S(2)}) copy-start(bf16[12]{0:T(256)(128)(2,1)} %param.24) | copy-start | bytes 76
  126.1 611.6 %copy-start.66 = (bf16[12]{0:T(256)(128)(2,1)S(1)}, bf16[12]{0:T(256)(128)(2,1)}, u32[]{:S(2)}) copy-start(bf16[12]{0:T(256)(128)(2,1)} %param.25) | copy-start | bytes 76
  126.1 611.9 %copy-start.58 = (bf16[832]{0:T(1024)(128)(2,1)S(1)}, bf16[832]{0:T(1024)(128)(2,1)}, u32[]{:S(2)}) copy-start(bf16[832]{0:T(1024)(128)(2,1)} %param.22) | copy-start | bytes 4996
  126.1 625.0 %copy-start.59 = (bf16[768]{0:T(1024)(128)(2,1)S(1)}, bf16[768]{0:T(1024)(128)(2,1)}, u32[]{:S(2)}) copy-start(bf16[768]{0:T(1024)(128)(2,1)} %param.27) | copy-start | bytes 4612
  135.1 629.9 %copy-start.12 = (bf16[1,256,1536]{2,1,0:T(8,128)(2,1)S(1)}, bf16[1,256,1536]{2,1,0:T(8,128)(2,1)}, u32[]{:S(2)}) copy-start(bf16[1,256,1536]{2,1,0:T(8,128)(2,1)} %param.16) | copy-start | bytes 2359300
  135.1 632.1 %collective-permute-start.3 = (bf16[2,384,6448]{1,2,0:T(8,128)(2,1)}, bf16[2,384,6448]{1,2,0:T(8,128)(2,1)}, u32[]{:S(2)}, u32[]{:S(2)}) collective-permute-start(bf16[2,384,6448]{1,2,0:T(8,128)(2,1)} %pad_maximum_fusion.1), channel_id=1, source_target_pairs={{0,2},{1,3},{2,0},{3,1},{4,6},{5,7},{6,4},{7,5},{8,10},{9,11},{10,... | collective-permute-start | bytes 29712392 | tf_op jit(solution)/shard_map/ppermute | solution.py:29
  137.9 1251.4 %reduce-scatter.8.cloned.1.call-start = ((), (), s32[]{:S(2)}) async-start(), calls=%async_computation.5 | async-start | bytes 23592960 | tf_op jit(solution)/shard_map/reduce_scatter | solution.py:286
  746.9 28.3 %copy-start.67 = (bf16[48]{0:T(256)(128)(2,1)}, bf16[48]{0:T(256)(128)(2,1)S(1)}, u32[]{:S(2)}) copy-start(bf16[48]{0:T(256)(128)(2,1)S(1)} %get-tuple-element.123) | copy-start | bytes 292
  750.1 85.0 %copy-start.39 = (f32[256]{0:T(256)}, f32[256]{0:T(256)S(1)}, u32[]{:S(2)}) copy-start(f32[256]{0:T(256)S(1)} %get-tuple-element.154) | copy-start | bytes 3076
  809.0 12.8 copy-start.48
  809.0 12.8 copy-start.60
  809.0 19.5 copy-start.46
  821.7 22.0 copy-start.11
  826.2 17.5 collective-permute-start.4
  830.1 13.6 copy-start.17
  833.6 10.1 copy-start.50
  867.9 5.8 collective-permute-start.1
  879.2 11.2 collective-permute-start.1
  895.8 13.6 collective-permute-start.1
  914.9 13.6 collective-permute-start.1
  934.0 13.6 collective-permute-start.1
  953.1 13.6 collective-permute-start.1
  972.2 13.6 collective-permute-start.1
  992.6 16.1 copy-start.9
  1025.5 1026.7 %reduce-scatter.6.cloned.1.call-start = ((), (), s32[]{:S(2)}) async-start(), calls=%async_computation.4 | async-start | bytes 49520640 | tf_op jit(solution)/shard_map/reduce_scatter | solution.py:285
  1032.2 8.4 copy-start.3
  1032.2 8.4 copy-start.5
  1032.2 8.4 copy-start.7
  1032.2 8.4 copy-start.42
  1032.2 8.4 copy-start.56
  1069.4 14.2 collective-permute-start
  1086.9 23.3 %collective-permute-start = (f32[48,64,128]{2,1,0:T(8,128)}, f32[48,64,128]{2,1,0:T(8,128)}, u32[]{:S(2)}, u32[]{:S(2)}) collective-permute-start(f32[48,64,128]{2,1,0:T(8,128)} %multiply_add_fusion.4), channel_id=1, source_target_pairs={{4,0},{8,4},{12,8},{16,12},{20,16},{24,20},{28,24},{5,1},{9,5},{13... | collective-permute-start | bytes 4718600 | tf_op jit(solution)/shard_map/while/body/eval_jaxpr/ppermute | solution.py:47
  1113.5 22.3 collective-permute-start
  1139.2 22.3 collective-permute-start
  1165.0 22.3 collective-permute-start
  1190.5 22.3 collective-permute-start
  1216.2 22.3 collective-permute-start
  1321.3 9.3 copy-start.18
  1321.3 10.8 copy-start.1
  1321.3 10.8 copy-start.19
  1323.1 15.6 copy-start.10
  1330.6 8.0 copy-start.8
  1330.6 8.0 copy-start.36
  1330.6 8.0 copy-start.37
  1344.7 8.2 copy-start.40
  1344.7 8.2 copy-start.49
  1344.7 8.2 copy-start.51
  1346.4 20.4 collective-permute-start.5
  1386.6 711.4 %reduce-scatter.10.cloned.1.call-start = ((), (), s32[]{:S(2)}) async-start(), calls=%async_computation.6 | async-start | bytes 2129920
  1389.2 905.5 %all-reduce.23.cloned.1.call-start = ((), (), s32[]{:S(2)}) async-start(), calls=%async_computation.7 | async-start | bytes 29245440 | tf_op jit(solution)/shard_map/psum | solution.py:296
  2062.7 11.2 copy-start.28
  2062.7 11.2 copy-start.44
  2062.7 11.2 copy-start.61
  2062.7 33.7 %copy-start.13 = (bf16[1,256,1536]{2,1,0:T(8,128)(2,1)S(1)}, bf16[1,256,1536]{2,1,0:T(8,128)(2,1)}, u32[]{:S(2)}) copy-start(bf16[1,256,1536]{2,1,0:T(8,128)(2,1)} %param.16) | copy-start | bytes 2359300
  2062.7 33.7 %copy-start.16 = (bf16[1,256,1536]{2,1,0:T(8,128)(2,1)S(1)}, bf16[1,256,1536]{2,1,0:T(8,128)(2,1)}, u32[]{:S(2)}) copy-start(bf16[1,256,1536]{2,1,0:T(8,128)(2,1)} %param.18) | copy-start | bytes 2359300
  2062.7 33.7 %copy-start.55 = (f32[256]{0:T(256)S(1)}, f32[256]{0:T(256)}, u32[]{:S(2)}) copy-start(f32[256]{0:T(256)} %get-tuple-element.159) | copy-start | bytes 3076
  2294.7 8.5 copy-start.14
  (29 other events, 98.7 us)
Sparse Core Ops, SparseCore 0:
  138.0 441.2 all-gather.4
  1025.6 328.9 reduce-scatter.7
  1386.8 665.3 reduce-scatter.5
  2055.0 40.8 reduce-scatter.9
  2100.0 194.6 all-reduce.22
